TPU v7x, 1024 devices: a whole 8x8x8 slice. The times are simulated.
1024 devices in a mesh: sub: 64 (over y, z), crs: 16 (over x, core).
Axes of the slice: x: 8, y: 8, z: 8, core: 2. Of those that a mesh axis runs over, the one named last changes fastest.
Arguments:
- jump_data: float32 [64, 16, 6, 384], P('sub', 'crs'), may hold values from -6 to 6
- lumped_scale: float32 [64, 16, 384], P('sub', 'crs'), may hold values from 0.3 to 3
- schur_inverse: float32 [64, 16, 768, 768], P('sub', 'crs'), as said below
- coarse_coupling: float32 [64, 16, 24, 768], P('sub', 'crs'), may hold values from -0.4375 to 0.4375
- corner_inverse: float32 [4096, 4096], P(None, 'crs'), as said below
- own_dof: int32 [64, 16, 384], P('sub', 'crs'), may hold values from 0 to 767, as said below
- nbr_dof: int32 [64, 16, 384], P('sub', 'crs'), may hold values from 0 to 767, as said below
- live_count: int32 [64, 16], P('sub', 'crs'), may hold values from 1 to 384, as said below
- corner_index: int32 [64, 16, 24], P('sub', 'crs'), may hold values from 0 to 4095
Outputs:
- multipliers: float32 [64, 16, 6, 384], P('sub', 'crs')
- residual: float32 [64, 16, 6, 384], P('sub', 'crs')
Inputs may be any that keep to these rules, and one draw needn't show every extreme that they name: `own_dof`: the 384 entries of one subdomain are distinct. `nbr_dof`: the 384 entries of one subdomain are distinct. `live_count`: some subdomain has all 384 slots live. `schur_inverse`: symmetric positive definite. `corner_inverse`: symmetric positive definite.
All inputs are finite; a program needn't handle non-finite values.
Results may differ from a plain program's by a relative error of at most 0.00021.
Values sent between devices are 32-bit elements; how exact they have to be, the bound alone decides.
A program may use at most 32 MiB of HBM per device.

v0:
```python
import jax
import jax.numpy as jnp
from jax import lax
from jax.sharding import Mesh
from jax.sharding import PartitionSpec as P

ITERS = 2
SUB_CRS = ("sub_0", "sub_1", "crs_0", "crs_1")
SUB = ("sub_0", "sub_1")
CRS = ("crs_0", "crs_1")


def over_axes(value, axes):
    for axis in axes:
        value = lax.psum(value, axis)
    return value


def passed_along(value, axis, steps):
    count = lax.axis_size(axis)
    pairs = [(source, (source + steps) % count) for source in range(count)]
    return lax.ppermute(value, axis, pairs)


def split_up(value, dim, count):
    shape = value.shape
    tiles = value.reshape(*shape[:dim], count, shape[dim] // count, *shape[dim + 1 :])
    return jnp.moveaxis(tiles, dim, 0)


def sum_at_owner(value, axis, dim):
    count = lax.axis_size(axis)
    tiles = lax.all_to_all(split_up(value, dim, count), axis, 0, 0, tiled=True)
    return jnp.sum(tiles, axis=0)


def copy_for_each(value, axis):
    copies = jnp.broadcast_to(value, (lax.axis_size(axis), *value.shape))
    return lax.all_to_all(copies, axis, split_axis=0, concat_axis=0, tiled=True)


def over_copies(value, axis):
    return copy_for_each(value, axis).sum(axis=0)


def in_order(tiles, dim):
    tiles = jnp.moveaxis(tiles, 0, dim)
    shape = tiles.shape
    return tiles.reshape(*shape[:dim], shape[dim] * shape[dim + 1], *shape[dim + 2 :])


def collect(value, axis, dim):
    return in_order(copy_for_each(value, axis), dim)


def product(left, right):
    return jnp.dot(left, right, precision=lax.Precision.HIGHEST, preferred_element_type=jnp.float32)


def paired_inner(residual, precon, image):
    return (
        over_axes(jnp.sum(residual * precon, axis=1), SUB_CRS),
        over_axes(jnp.sum(precon * image, axis=1), SUB_CRS),
    )


def per_device(
    jump_data,
    lumped_scale,
    schur_inverse,
    coarse_coupling,
    corner_inverse,
    own_dof,
    nbr_dof,
    live_count,
    corner_index,
):
    given = jump_data[0, 0]
    scale = lumped_scale[0, 0][None, :]
    schur = schur_inverse[0, 0]
    coupling = coarse_coupling[0, 0]
    records = given.shape[1]
    iface = schur.shape[0]
    corners = corner_inverse.shape[0]
    live = (jnp.arange(records, dtype=jnp.int32) < live_count[0, 0]).astype(jnp.float32)
    columns = jnp.arange(iface, dtype=jnp.int32)[None, :]
    own_map = (own_dof[0, 0][:, None] == columns).astype(jnp.float32) * live[:, None]
    next_map = (nbr_dof[0, 0][:, None] == columns).astype(jnp.float32) * live[:, None]
    corner_map = (
        corner_index[0, 0][:, None] == jnp.arange(corners, dtype=jnp.int32)[None, :]
    ).astype(jnp.float32)

    def operate(field):
        own_load = product(field, own_map)
        next_load = product(field, next_map)
        from_left = passed_along(next_load, SUB, 1)
        load = own_load - from_left
        local_part = product(load, schur)
        corner_force = product(load, coupling.T)
        spread = product(corner_force, corner_map)
        chain_rows = sum_at_owner(spread, CRS, 1)
        corner_total = over_copies(chain_rows, SUB)
        whole_force = collect(corner_total, CRS, 1)
        solution_share = product(whole_force, corner_inverse)
        corner_solution = collect(solution_share, CRS, 1)
        picked = product(corner_solution, corner_map.T)
        displacement = local_part + product(picked, coupling)
        from_right = passed_along(displacement, SUB, -1)
        return product(displacement, own_map.T) - product(from_right, next_map.T)

    residual = given * live[None, :]
    multipliers = jnp.zeros_like(residual)
    precon = scale * residual
    image = operate(precon)
    norm_now, curvature = paired_inner(residual, precon, image)
    alpha = norm_now / curvature
    direction, along = (precon, image)
    for step in range(ITERS):
        multipliers = multipliers + alpha[:, None] * direction
        residual = residual - alpha[:, None] * along
        if step + 1 < ITERS:
            precon = scale * residual
            image = operate(precon)
            norm_next, curvature = paired_inner(residual, precon, image)
            ratio = norm_next / norm_now
            alpha = norm_next / (curvature - ratio * norm_next / alpha)
            direction = precon + ratio[:, None] * direction
            along = image + ratio[:, None] * along
            norm_now = norm_next
    return (multipliers[None, None], residual[None, None])


def solution(mesh):
    finer = Mesh(mesh.devices.reshape(8, 8, 8, 2), ("sub_0", "sub_1", "crs_0", "crs_1"))
    placed = (
        P(SUB, CRS, None, None),
        P(SUB, CRS, None),
        P(SUB, CRS, None, None),
        P(SUB, CRS, None, None),
        P(None, CRS),
        P(SUB, CRS, None),
        P(SUB, CRS, None),
        P(SUB, CRS),
        P(SUB, CRS, None),
    )
    return jax.shard_map(
        per_device,
        mesh=finer,
        in_specs=placed,
        out_specs=(P(SUB, CRS, None, None), P(SUB, CRS, None, None)),
        check_vma=False,
    )
```

profile of v0, /device:TPU:1, one launch (start us, length us, event | category | flops | bytes accessed | tf_op | source)
XLA Modules:
  0.0 296.7 jit_solution(12740371568054573321)
XLA Ops:
  2.9 1.5 fusion.10
  4.4 5.7 %collective-permute-start = (f32[6,768]{1,0:T(8,128)S(1)}, f32[6,768]{1,0:T(8,128)S(1)}, u32[]{:S(2)}, u32[]{:S(2)}) collective-permute-start(f32[6,768]{1,0:T(8,128)S(1)} %fusion.10), channel_id=1, source_target_pairs={{0,16},{16,32},{32,48},{48,64},{64,80},{80,96},{96,112},{112,128},... | collective-permute-start | bytes 55304 | tf_op jit(solution)/shard_map/ppermute | solution.py:22
  10.8 16.3 %collective-permute-done = f32[6,768]{1,0:T(8,128)S(1)} collective-permute-done((f32[6,768]{1,0:T(8,128)S(1)}, f32[6,768]{1,0:T(8,128)S(1)}, u32[]{:S(2)}, u32[]{:S(2)}) %collective-permute-start) | collective-permute-done | bytes 18464 | tf_op jit(solution)/shard_map/ppermute | solution.py:22
  27.2 1.5 fusion.20
  29.2 17.0 %all_to_all.40 = f32[16,6,256]{2,1,0:T(8,128)S(1)} all-to-all(f32[16,6,256]{2,1,0:T(8,128)S(1)} %bitcast.79), channel_id=1, replica_groups=mesh['sub_0'=8,'sub_1'=8,'crs_0'=8,'crs_1'=2] {'crs_0','crs_1'}, dimensions={0} | all-to-all | bytes 196608 | tf_op jit(solution)/shard_map/all_to_all | solution.py:33
  46.2 23.4 %all_to_all.41 = f32[64,6,256]{2,1,0:T(8,128)S(1)} all-to-all(f32[64,6,256]{2,1,0:T(8,128)S(1)} %broadcast_in_dim.16), channel_id=1, replica_groups=mesh['sub_0'=8,'sub_1'=8,'crs_0'=8,'crs_1'=2] {'sub_0','sub_1'}, dimensions={0} | all-to-all | bytes 786432 | tf_op jit(solution)/shard_map/all_to_all | solution.py:39
  69.7 13.5 %all_to_all.42 = f32[16,6,256]{2,1,0:T(8,128)S(1)} all-to-all(f32[16,6,256]{2,1,0:T(8,128)S(1)} %broadcast_in_dim.17), channel_id=1, replica_groups=mesh['sub_0'=8,'sub_1'=8,'crs_0'=8,'crs_1'=2] {'crs_0','crs_1'}, dimensions={0} | all-to-all | bytes 196608 | tf_op jit(solution)/shard_map/all_to_all | solution.py:39
  83.2 3.9 %fusion.105 = f32[6,256]{1,0:T(8,128)S(1)} fusion(f32[6,4096]{1,0:T(8,128)S(1)} %bitcast.77, f32[4096,256]{1,0:T(8,128)} %param.13), kind=kOutput, calls=%fused_computation.107 | convolution fusion | flops 75497472 | bytes 4298752 | tf_op jit(solution)/shard_map/dot_general | solution.py:57
  87.2 11.6 %all_to_all.43 = f32[16,6,256]{2,1,0:T(8,128)S(1)} all-to-all(f32[16,6,256]{2,1,0:T(8,128)S(1)} %broadcast_in_dim.18), channel_id=1, replica_groups=mesh['sub_0'=8,'sub_1'=8,'crs_0'=8,'crs_1'=2] {'crs_0','crs_1'}, dimensions={0} | all-to-all | bytes 196608 | tf_op jit(solution)/shard_map/all_to_all | solution.py:39
  99.3 1.2 fusion.26
  100.5 3.1 %collective-permute-start.1 = (f32[6,768]{1,0:T(8,128)S(1)}, f32[6,768]{1,0:T(8,128)S(1)}, u32[]{:S(2)}, u32[]{:S(2)}) collective-permute-start(f32[6,768]{1,0:T(8,128)S(1)} %fusion.26), channel_id=1, source_target_pairs={{0,1008},{16,0},{32,16},{48,32},{64,48},{80,64},{96,80},{112,96},{... | collective-permute-start | bytes 55304 | tf_op jit(solution)/shard_map/ppermute | solution.py:22
  103.6 1.2 fusion.16
  105.1 1.3 fusion.83
  106.4 12.7 %all-reduce.5 = (f32[6]{0:T(128)S(1)}, f32[6]{0:T(128)S(1)}) all-reduce(f32[6]{0:T(128)S(1)} %get-tuple-element.13, f32[6]{0:T(128)S(1)} %get-tuple-element.12), channel_id=1, replica_groups=mesh['sub_0'=8,'sub_1'=8,'crs_0'=8,'crs_1'=2] {'sub_0'}, use_global_device_ids=true, to_apply=%region_1.0 | all-reduce | flops 12 | bytes 96 | tf_op jit(solution)/shard_map/psum | solution.py:15
  119.1 13.5 %all-reduce.3 = (f32[6]{0:T(128)S(1)}, f32[6]{0:T(128)S(1)}) all-reduce(f32[6]{0:T(128)S(1)} %get-tuple-element.24, f32[6]{0:T(128)S(1)} %get-tuple-element.25), channel_id=1, replica_groups=mesh['sub_0'=8,'sub_1'=8,'crs_0'=8,'crs_1'=2] {'sub_1'}, use_global_device_ids=true, to_apply=%region_2.0 | all-reduce | flops 12 | bytes 96 | tf_op jit(solution)/shard_map/psum | solution.py:15
  132.6 11.5 %all-reduce.1 = (f32[6]{0:T(128)S(1)}, f32[6]{0:T(128)S(1)}) all-reduce(f32[6]{0:T(128)S(1)} %get-tuple-element.20, f32[6]{0:T(128)S(1)} %get-tuple-element.21), channel_id=1, replica_groups=mesh['sub_0'=8,'sub_1'=8,'crs_0'=8,'crs_1'=2] {'crs_0'}, use_global_device_ids=true, to_apply=%region_3.0 | all-reduce | flops 12 | bytes 96 | tf_op jit(solution)/shard_map/psum | solution.py:15
  144.2 13.9 %all-reduce.7 = (f32[6]{0:T(128)S(1)}, f32[6]{0:T(128)S(1)}) all-reduce(f32[6]{0:T(128)S(1)} %get-tuple-element.16, f32[6]{0:T(128)S(1)} %get-tuple-element.17), channel_id=1, replica_groups=mesh['sub_0'=8,'sub_1'=8,'crs_0'=8,'crs_1'=2] {'crs_1'}, use_global_device_ids=true, to_apply=%region_4.0 | all-reduce | flops 12 | bytes 96 | tf_op jit(solution)/shard_map/psum | solution.py:15
  159.0 1.9 collective-permute-start.2
  160.9 6.0 %collective-permute-done.2 = f32[6,768]{1,0:T(8,128)S(1)} collective-permute-done((f32[6,768]{1,0:T(8,128)S(1)}, f32[6,768]{1,0:T(8,128)S(1)}, u32[]{:S(2)}, u32[]{:S(2)}) %collective-permute-start.2) | collective-permute-done | bytes 18464 | tf_op jit(solution)/shard_map/ppermute | solution.py:22
  168.2 14.8 %all_to_all.44 = f32[16,6,256]{2,1,0:T(8,128)S(1)} all-to-all(f32[16,6,256]{2,1,0:T(8,128)S(1)} %bitcast.80), channel_id=1, replica_groups=mesh['sub_0'=8,'sub_1'=8,'crs_0'=8,'crs_1'=2] {'crs_0','crs_1'}, dimensions={0} | all-to-all | bytes 196608 | tf_op jit(solution)/shard_map/all_to_all | solution.py:33
  183.1 23.8 %all_to_all.45 = f32[64,6,256]{2,1,0:T(8,128)S(1)} all-to-all(f32[64,6,256]{2,1,0:T(8,128)S(1)} %broadcast_in_dim.38), channel_id=1, replica_groups=mesh['sub_0'=8,'sub_1'=8,'crs_0'=8,'crs_1'=2] {'sub_0','sub_1'}, dimensions={0} | all-to-all | bytes 786432 | tf_op jit(solution)/shard_map/all_to_all | solution.py:39
  207.0 13.5 %all_to_all.46 = f32[16,6,256]{2,1,0:T(8,128)S(1)} all-to-all(f32[16,6,256]{2,1,0:T(8,128)S(1)} %broadcast_in_dim.39), channel_id=1, replica_groups=mesh['sub_0'=8,'sub_1'=8,'crs_0'=8,'crs_1'=2] {'crs_0','crs_1'}, dimensions={0} | all-to-all | bytes 196608 | tf_op jit(solution)/shard_map/all_to_all | solution.py:39
  220.6 3.9 %fusion.106 = f32[6,256]{1,0:T(8,128)S(1)} fusion(f32[6,4096]{1,0:T(8,128)S(1)} %bitcast.78, f32[4096,256]{1,0:T(8,128)} %param.13), kind=kOutput, calls=%fused_computation.108 | convolution fusion | flops 75497472 | bytes 4298752 | tf_op jit(solution)/shard_map/dot_general | solution.py:57
  224.5 11.6 %all_to_all.47 = f32[16,6,256]{2,1,0:T(8,128)S(1)} all-to-all(f32[16,6,256]{2,1,0:T(8,128)S(1)} %broadcast_in_dim.40), channel_id=1, replica_groups=mesh['sub_0'=8,'sub_1'=8,'crs_0'=8,'crs_1'=2] {'crs_0','crs_1'}, dimensions={0} | all-to-all | bytes 196608 | tf_op jit(solution)/shard_map/all_to_all | solution.py:39
  236.6 1.2 fusion.29
  237.8 3.1 %collective-permute-start.3 = (f32[6,768]{1,0:T(8,128)S(1)}, f32[6,768]{1,0:T(8,128)S(1)}, u32[]{:S(2)}, u32[]{:S(2)}) collective-permute-start(f32[6,768]{1,0:T(8,128)S(1)} %fusion.29), channel_id=1, source_target_pairs={{0,1008},{16,0},{32,16},{48,32},{64,48},{80,64},{96,80},{112,96},{... | collective-permute-start | bytes 55304 | tf_op jit(solution)/shard_map/ppermute | solution.py:22
  240.9 1.2 fusion.12
  242.4 1.3 fusion.87
  243.7 12.7 %all-reduce.4 = (f32[6]{0:T(128)S(1)}, f32[6]{0:T(128)S(1)}) all-reduce(f32[6]{0:T(128)S(1)} %get-tuple-element.11, f32[6]{0:T(128)S(1)} %get-tuple-element.10), channel_id=1, replica_groups=mesh['sub_0'=8,'sub_1'=8,'crs_0'=8,'crs_1'=2] {'sub_0'}, use_global_device_ids=true, to_apply=%region_13.0 | all-reduce | flops 12 | bytes 96 | tf_op jit(solution)/shard_map/psum | solution.py:15
  256.4 13.5 %all-reduce.2 = (f32[6]{0:T(128)S(1)}, f32[6]{0:T(128)S(1)}) all-reduce(f32[6]{0:T(128)S(1)} %get-tuple-element.22, f32[6]{0:T(128)S(1)} %get-tuple-element.23), channel_id=1, replica_groups=mesh['sub_0'=8,'sub_1'=8,'crs_0'=8,'crs_1'=2] {'sub_1'}, use_global_device_ids=true, to_apply=%region_14.0 | all-reduce | flops 12 | bytes 96 | tf_op jit(solution)/shard_map/psum | solution.py:15
  269.9 11.5 %all-reduce = (f32[6]{0:T(128)S(1)}, f32[6]{0:T(128)S(1)}) all-reduce(f32[6]{0:T(128)S(1)} %get-tuple-element.18, f32[6]{0:T(128)S(1)} %get-tuple-element.19), channel_id=1, replica_groups=mesh['sub_0'=8,'sub_1'=8,'crs_0'=8,'crs_1'=2] {'crs_0'}, use_global_device_ids=true, to_apply=%region_15.0 | all-reduce | flops 12 | bytes 96 | tf_op jit(solution)/shard_map/psum | solution.py:15
  281.5 13.9 %all-reduce.6 = (f32[6]{0:T(128)S(1)}, f32[6]{0:T(128)S(1)}) all-reduce(f32[6]{0:T(128)S(1)} %get-tuple-element.14, f32[6]{0:T(128)S(1)} %get-tuple-element.15), channel_id=1, replica_groups=mesh['sub_0'=8,'sub_1'=8,'crs_0'=8,'crs_1'=2] {'crs_1'}, use_global_device_ids=true, to_apply=%region_16.0 | all-reduce | flops 12 | bytes 96 | tf_op jit(solution)/shard_map/psum | solution.py:15
  (40 shorter events, 8.2 us)
Async XLA Ops:
  0.6 98.7 %copy-start = (f32[1,1,768,768]{3,2,1,0:T(8,128)S(1)}, f32[1,1,768,768]{3,2,1,0:T(8,128)}, u32[]{:S(2)}) copy-start(f32[1,1,768,768]{3,2,1,0:T(8,128)} %param.11) | copy-start | bytes 7077892
  0.6 28.0 %copy-start.1 = (f32[1,1,24,768]{3,2,1,0:T(8,128)S(1)}, f32[1,1,24,768]{3,2,1,0:T(8,128)}, u32[]{:S(2)}) copy-start(f32[1,1,24,768]{3,2,1,0:T(8,128)} %param.12) | copy-start | bytes 221188
  0.7 28.2 %copy-start.3 = (s32[1,1,24]{2,1,0:T(1,128)S(1)}, s32[1,1,24]{2,1,0:T(1,128)}, u32[]{:S(2)}) copy-start(s32[1,1,24]{2,1,0:T(1,128)} %param.17) | copy-start | bytes 292
  4.4 22.8 %collective-permute-start = (f32[6,768]{1,0:T(8,128)S(1)}, f32[6,768]{1,0:T(8,128)S(1)}, u32[]{:S(2)}, u32[]{:S(2)}) collective-permute-start(f32[6,768]{1,0:T(8,128)S(1)} %fusion.10), channel_id=1, source_target_pairs={{0,16},{16,32},{32,48},{48,64},{64,80},{80,96},{96,112},{112,128},... | collective-permute-start | bytes 55304 | tf_op jit(solution)/shard_map/ppermute | solution.py:22
  99.3 5.8 %copy-start.2 = (f32[1,1,6,384]{3,1,2,0:T(1,128)S(1)}, f32[1,1,6,384]{3,1,2,0:T(1,128)}, u32[]{:S(2)}) copy-start(f32[1,1,6,384]{3,1,2,0:T(1,128)} %param.9) | copy-start | bytes 27652
  100.5 4.6 %collective-permute-start.1 = (f32[6,768]{1,0:T(8,128)S(1)}, f32[6,768]{1,0:T(8,128)S(1)}, u32[]{:S(2)}, u32[]{:S(2)}) collective-permute-start(f32[6,768]{1,0:T(8,128)S(1)} %fusion.26), channel_id=1, source_target_pairs={{0,1008},{16,0},{32,16},{48,32},{64,48},{80,64},{96,80},{112,96},{... | collective-permute-start | bytes 55304 | tf_op jit(solution)/shard_map/ppermute | solution.py:22
  159.0 7.9 %collective-permute-start.2 = (f32[6,768]{1,0:T(8,128)S(1)}, f32[6,768]{1,0:T(8,128)S(1)}, u32[]{:S(2)}, u32[]{:S(2)}) collective-permute-start(f32[6,768]{1,0:T(8,128)S(1)} %fusion.6), channel_id=1, source_target_pairs={{0,16},{16,32},{32,48},{48,64},{64,80},{80,96},{96,112},{112,128},... | collective-permute-start | bytes 55304 | tf_op jit(solution)/shard_map/ppermute | solution.py:22
  237.8 4.6 %collective-permute-start.3 = (f32[6,768]{1,0:T(8,128)S(1)}, f32[6,768]{1,0:T(8,128)S(1)}, u32[]{:S(2)}, u32[]{:S(2)}) collective-permute-start(f32[6,768]{1,0:T(8,128)S(1)} %fusion.29), channel_id=1, source_target_pairs={{0,1008},{16,0},{32,16},{48,32},{64,48},{80,64},{96,80},{112,96},{... | collective-permute-start | bytes 55304 | tf_op jit(solution)/shard_map/ppermute | solution.py:22
where the time goes:
time: 298 us; the launch traced here: 297 us
  blocking collectives  233 us (78%)
  waiting for transfers between devices  22.9 us (8%)
  matrix products  22 us (7%)
  starting transfers between devices  13.8 us (5%)
    psum x8, blocking collectives, over_axes(): value = lax.psum(value, axis)  103 us
    all_to_all x6, blocking collectives, copy_for_each(): return lax.all_to_all(copies, axis, split_axis=0, concat_axis=0, tiled=True)  97.4 us
    all_to_all x2, blocking collectives, sum_at_owner(): tiles = lax.all_to_all(split_up(value, dim, count), axis, 0, 0, tiled=True)  31.8 us
    ppermute x4, waiting for transfers between devices, passed_along(): return lax.ppermute(value, axis, pairs)  22.9 us
    dot_general x20, matrix products, product(): jnp.dot(left, right, precision=lax.Precision.HIGHEST, preferred_element_t...  22 us
    ppermute x4, starting transfers between devices, passed_along(): return lax.ppermute(value, axis, pairs)  13.8 us
  transfers between devices with their start and end apart: 4, of which 4 were waited for; matrix products, arithmetic and copies ran while one was open for 1% of the time, Pallas kernels for 0%

commit v1 on v0

v1 whole, which is shorter than its diff:
```python
import functools

import jax
import jax.numpy as jnp
from jax import lax
from jax.experimental import pallas as pl
from jax.experimental.pallas import tpu as pltpu
from jax.sharding import Mesh
from jax.sharding import PartitionSpec as P

MESH = pl.DeviceIdType.MESH
LANES = 128
ROWS = 8
F32 = jnp.float32
BF16 = jnp.bfloat16
CONTRACT_LAST = (((1,), (1,)), ((), ()))
CONTRACT = (((1,), (0,)), ((), ()))


def parts(value):
    high = value.astype(BF16).astype(F32)
    rest = value - high
    middle = rest.astype(BF16).astype(F32)
    low = rest - middle
    return jnp.concatenate([high, middle, low], axis=0).astype(BF16)


def times(value, matrices, dims):
    rows = value.shape[0]
    stacked = parts(value)
    total = None
    for matrix in matrices:
        found = lax.dot_general(stacked, matrix, dims, preferred_element_type=F32)
        total = found if total is None else total + found
    return total[:rows] + total[rows : 2 * rows] + total[2 * rows :]


def store_split(value, high_ref, low_ref):
    high = value.astype(BF16)
    high_ref[...] = high
    low_ref[...] = (value - high.astype(F32)).astype(BF16)


def kernel(
    ny,
    nz,
    nx,
    nk,
    given_ref,
    scale_ref,
    coupling_ref,
    own_ref,
    nbr_ref,
    index_ref,
    live_ref,
    schur_hbm,
    inverse_hbm,
    mult_ref,
    res_ref,
    schur,
    inverse,
    schur_high,
    schur_low,
    own_map,
    next_map,
    corner_map,
    rows_of,
    rows_high,
    rows_low,
    own_wide,
    pair_wide,
    pair_high,
    pair_low,
    index_pad,
    index_right,
    index_mine,
    index_line,
    index_rows,
    index_smem,
    coupling_right,
    load_send,
    load_recv,
    disp_send,
    disp_recv,
    force_send,
    force_recv,
    pick_send,
    pick_recv,
    sum_y0,
    sum_z0,
    sum_y1,
    sum_z1,
    local_sem,
    near_send,
    near_recv,
    index_send_sem,
    index_recv_sem,
    force_send_sem,
    force_recv_sem,
    pick_send_sem,
    pick_recv_sem,
    y_send_sem,
    y_recv_sem,
    z_send_sem,
    z_recv_sem,
):
    y, z, x, k = (lax.axis_index(a) for a in ("y", "z", "x", "k"))
    slab = x * nk + k
    slabs = nx * nk
    iface = coupling_ref.shape[1]
    corners = coupling_ref.shape[0]
    records = given_ref.shape[1]
    block = inverse.shape[1]
    half = LANES // nk

    def plus(value, step, count):
        return lax.rem(value + step + count, count)

    right_z = plus(z, 1, nz)
    right_y = plus(y, jnp.where(z == nz - 1, 1, 0), ny)
    left_z = plus(z, -1, nz)
    left_y = plus(y, jnp.where(z == 0, -1, 0), ny)
    right = {"y": right_y, "z": right_z}
    left = {"y": left_y, "z": left_z}

    def by_distance(count):
        return sorted(range(1, count), key=lambda d: -min(d, count - d))

    line = []
    for dx in sorted(range(nx), key=lambda d: -min(d, nx - d)):
        for dk in range(nk):
            if dx or dk:
                line.append((plus(x, dx, nx), plus(k, dk, nk)))
    ys = [plus(y, d, ny) for d in by_distance(ny)]
    zs = [plus(z, d, nz) for d in by_distance(nz)]

    barrier = pltpu.get_barrier_semaphore()
    everyone = [{"x": px, "k": pk} for px, pk in line]
    everyone += [{"y": py} for py in ys] + [{"z": pz} for pz in zs] + [left, right]
    for peer in everyone:
        pl.semaphore_signal(barrier, inc=1, device_id=peer, device_id_type=MESH)

    get_schur = pltpu.make_async_copy(schur_hbm, schur, local_sem.at[0])
    get_inverse = pltpu.make_async_copy(inverse_hbm, inverse, local_sem.at[1])
    get_schur.start()
    get_inverse.start()

    started = []

    def send(source, target, send_sem, recv_sem, device):
        copy = pltpu.make_async_remote_copy(
            src_ref=source,
            dst_ref=target,
            send_sem=send_sem,
            recv_sem=recv_sem,
            device_id=device,
            device_id_type=MESH,
        )
        copy.start()
        started.append(copy)

    def arrive(target, send_sem, recv_sem, device):
        pltpu.make_async_remote_copy(
            src_ref=target,
            dst_ref=target,
            send_sem=send_sem,
            recv_sem=recv_sem,
            device_id=device,
            device_id_type=MESH,
        ).wait_recv()

    def spread_line(sources, target, send_sem, recv_sem):
        for slot, (px, pk) in enumerate(line):
            send(sources(px), target.at[slab], send_sem.at[slot], recv_sem.at[slab], {"x": px, "k": pk})

    def await_line(target, send_sem, recv_sem):
        for px, pk in line:
            peer = px * nk + pk
            arrive(target.at[peer], send_sem.at[0], recv_sem.at[peer], {"x": px, "k": pk})

    def spread_axis(buffer, axis, me, peers, send_sem, recv_sem):
        for slot, peer in enumerate(peers):
            send(buffer.at[me], buffer.at[me], send_sem.at[slot], recv_sem.at[me], {axis: peer})

    def await_axis(buffer, axis, peers, send_sem, recv_sem):
        for peer in peers:
            arrive(buffer.at[peer], send_sem.at[0], recv_sem.at[peer], {axis: peer})

    def added(buffer, count):
        total = buffer[0]
        for slot in range(1, count):
            total = total + buffer[slot]
        return total

    def padded(value):
        return jnp.concatenate([value, jnp.zeros((ROWS - value.shape[0], value.shape[1]), F32)], axis=0)

    live_row = lax.broadcasted_iota(jnp.int32, (1, records), 1) < live_ref[0, 0]
    residual0 = padded(given_ref[...]) * live_row.astype(F32)
    scale = scale_ref[...]
    direction0 = residual0 * scale
    rows_iface = lax.broadcasted_iota(jnp.int32, (iface, records), 0)
    own_map[...] = jnp.where((rows_iface == own_ref[...]) & live_row, 1.0, 0.0).astype(BF16)
    next_map[...] = jnp.where((rows_iface == nbr_ref[...]) & live_row, 1.0, 0.0).astype(BF16)
    load_send[0] = times(direction0, (next_map[...],), CONTRACT_LAST)
    index_pad[...] = jnp.full((ROWS, LANES), -1, jnp.int32)
    index_pad[0:1, 0:corners] = index_ref[...]

    pl.semaphore_wait(barrier, len(everyone))

    send(load_send.at[0], load_recv.at[0], near_send.at[0], near_recv.at[0], right)
    send(index_pad, index_right, near_send.at[1], near_recv.at[1], left)
    send(coupling_ref, coupling_right, near_send.at[2], near_recv.at[2], left)

    own_load0 = times(direction0, (own_map[...],), CONTRACT_LAST)
    own_wide[...] = jnp.zeros_like(own_wide)
    pair_wide[...] = jnp.zeros_like(pair_wide)
    rows_of[...] = jnp.zeros_like(rows_of)
    first = pl.multiple_of(k * half, 8)
    second = pl.multiple_of(k * half + corners, 8)
    coupling = coupling_ref[...]
    own_wide[pl.ds(first, corners), :] = coupling
    wide_high = own_wide[...].astype(BF16)
    wide_low = (own_wide[...] - wide_high.astype(F32)).astype(BF16)
    pair_wide[pl.ds(first, corners), :] = times(coupling, (own_map[...],), CONTRACT)

    arrive(index_right, near_send.at[1], near_recv.at[1], right)
    lane = lax.broadcasted_iota(jnp.int32, (ROWS, LANES), 1)
    both = jnp.where(lane < corners, index_pad[...], pltpu.roll(index_right[...], corners, 1))
    both = jnp.where(lane < 2 * corners, both, -1)
    for other in range(1, nk):
        both = jnp.where(k == other, pltpu.roll(both, other * half, 1), both)
    index_mine[...] = both
    spread_line(lambda px: index_mine, index_line, index_send_sem, index_recv_sem)

    arrive(load_recv.at[0], near_send.at[0], near_recv.at[0], left)
    load0 = own_load0 - load_recv[0]
    force = times(load0, (wide_high, wide_low), CONTRACT_LAST)
    force_send[0] = force
    spread_line(lambda px: force_send.at[0], force_recv.at[0], force_send_sem.at[0], force_recv_sem.at[0])

    get_schur.wait()
    store_split(schur[...], schur_high, schur_low)
    disp0 = times(load0, (schur_high[...], schur_low[...]), CONTRACT)
    disp_send[0] = disp0
    send(disp_send.at[0], disp_recv.at[0], near_send.at[3], near_recv.at[3], left)
    arrive(coupling_right, near_send.at[2], near_recv.at[2], right)
    pair_wide[pl.ds(second, corners), :] = -times(coupling_right[...], (next_map[...],), CONTRACT)
    store_split(pair_wide[...], pair_high, pair_low)

    await_line(index_line, index_send_sem, index_recv_sem)
    index_line[slab] = index_mine[...]
    block_rows = lax.broadcasted_iota(jnp.int32, (block, LANES), 0) + slab * block
    for px in range(nx):
        row = index_line[px * nk]
        for pk in range(1, nk):
            row = jnp.maximum(row, index_line[px * nk + pk])
        row = row[0:1]
        index_rows[px : px + 1, :] = row
        corner_map[:, px * LANES : (px + 1) * LANES] = jnp.where(block_rows == row, 1.0, 0.0).astype(BF16)
    to_smem = pltpu.make_async_copy(index_rows, index_smem, local_sem.at[2])
    to_smem.start()

    def line_force(step):
        force_recv[step, slab] = force_send[step]
        tiles = []
        for px in range(nx):
            tile = force_recv[step, px * nk]
            for pk in range(1, nk):
                tile = tile + force_recv[step, px * nk + pk]
            tiles.append(tile)
        return jnp.concatenate(tiles, axis=1)

    def send_picks(step, picks):
        for px in range(nx):
            pick_send[step, px] = picks[:, px * LANES : (px + 1) * LANES]
        pick_recv[step, slab] = pick_send[step, x]
        spread_line(
            lambda px: pick_send.at[step, px], pick_recv.at[step], pick_send_sem.at[step], pick_recv_sem.at[step]
        )

    def get_picks(step):
        await_line(pick_recv.at[step], pick_send_sem.at[step], pick_recv_sem.at[step])
        return added(pick_recv.at[step], slabs)

    await_line(force_recv.at[0], force_send_sem.at[0], force_recv_sem.at[0])
    sum_y0[y] = times(line_force(0), (corner_map[...],), CONTRACT_LAST)
    spread_axis(sum_y0, "y", y, ys, y_send_sem.at[0], y_recv_sem.at[0])

    get_inverse.wait()
    to_smem.wait()

    def take(j, carry):
        for px in range(nx):
            for pk in range(nk):
                at = index_smem[px, pk * half + j]
                rows_of[pl.ds(px * LANES + pk * half + j, 1), :] = inverse[pl.ds(at, 1), :]
        return carry

    lax.fori_loop(0, 2 * corners, take, 0)
    store_split(rows_of[...], rows_high, rows_low)

    await_axis(sum_y0, "y", ys, y_send_sem.at[0], y_recv_sem.at[0])
    sum_z0[z] = added(sum_y0, ny)
    spread_axis(sum_z0, "z", z, zs, z_send_sem.at[0], z_recv_sem.at[0])
    arrive(disp_recv.at[0], near_send.at[3], near_recv.at[3], right)
    local0 = times(disp0, (own_map[...],), CONTRACT) - times(disp_recv[0], (next_map[...],), CONTRACT)
    await_axis(sum_z0, "z", zs, z_send_sem.at[0], z_recv_sem.at[0])
    total0 = added(sum_z0, nz)
    send_picks(0, times(total0, (rows_high[...], rows_low[...]), CONTRACT_LAST))
    solved0 = get_picks(0)
    image0 = local0 + times(solved0, (pair_high[...], pair_low[...]), CONTRACT)

    scaled = image0 * scale
    load_send[1] = times(scaled, (next_map[...],), CONTRACT_LAST)
    send(load_send.at[1], load_recv.at[1], near_send.at[4], near_recv.at[4], right)
    force_send[1] = times(scaled, (pair_high[...], pair_low[...]), CONTRACT_LAST)
    spread_line(lambda px: force_send.at[1], force_recv.at[1], force_send_sem.at[1], force_recv_sem.at[1])
    own_load1 = times(scaled, (own_map[...],), CONTRACT_LAST)

    def inner(first_value, second_value):
        return jnp.sum(first_value * second_value, axis=1, keepdims=True)

    start_norm = inner(residual0, direction0)
    curvature = inner(direction0, image0)
    scaled_norm = inner(image0, scaled)
    arrive(load_recv.at[1], near_send.at[4], near_recv.at[4], left)
    load1 = own_load1 - load_recv[1]
    disp1 = times(load1, (schur_high[...], schur_low[...]), CONTRACT)
    disp_send[1] = disp1
    send(disp_send.at[1], disp_recv.at[1], near_send.at[5], near_recv.at[5], left)
    energy = inner(load1, disp1)
    sums = jnp.where(
        lane == 0,
        start_norm,
        jnp.where(lane == 1, curvature, jnp.where(lane == 2, scaled_norm, jnp.where(lane == 3, energy, 0.0))),
    )
    await_line(force_recv.at[1], force_send_sem.at[1], force_recv_sem.at[1])
    forces = line_force(1)
    sum_y1[y, :, 0:block] = times(forces, (corner_map[...],), CONTRACT_LAST)
    sum_y1[y, :, block : 2 * block] = times(forces, (rows_high[...], rows_low[...]), CONTRACT)
    sum_y1[y, :, 2 * block :] = sums
    spread_axis(sum_y1, "y", y, ys, y_send_sem.at[1], y_recv_sem.at[1])
    await_axis(sum_y1, "y", ys, y_send_sem.at[1], y_recv_sem.at[1])
    sum_z1[z] = added(sum_y1, ny)
    spread_axis(sum_z1, "z", z, zs, z_send_sem.at[1], z_recv_sem.at[1])
    arrive(disp_recv.at[1], near_send.at[5], near_recv.at[5], right)
    local1 = times(disp1, (own_map[...],), CONTRACT) - times(disp_recv[1], (next_map[...],), CONTRACT)
    await_axis(sum_z1, "z", zs, z_send_sem.at[1], z_recv_sem.at[1])
    total1 = added(sum_z1, nz)
    solved_block = total1[:, block : 2 * block]
    sums = total1[:, 2 * block :]
    sums = sums + jnp.where(lane == 3, inner(total1[:, 0:block], solved_block), 0.0)
    picks = times(solved_block, (corner_map[...],), CONTRACT)
    sums = pltpu.roll(sums, LANES - half // 4, 1)
    send_picks(1, picks + jnp.concatenate([sums] * nx, axis=1))
    solved1 = get_picks(1)
    image1 = local1 + times(solved1, (pair_high[...], pair_low[...]), CONTRACT)

    at = LANES - half // 4
    norm0 = solved1[:, at : at + 1]
    alpha0 = norm0 / solved1[:, at + 1 : at + 2]
    norm1 = alpha0 * alpha0 * solved1[:, at + 2 : at + 3] - norm0
    ratio = norm1 / norm0
    bent = alpha0 * alpha0 * solved1[:, at + 3 : at + 4] - (norm0 + norm1) * (1.0 + ratio) / alpha0
    alpha1 = norm1 / bent
    residual1 = residual0 - alpha0 * image0
    direction1 = residual1 * scale + ratio * direction0
    along1 = image0 - alpha0 * image1 + ratio * image0
    cases = mult_ref.shape[0]
    mult_ref[...] = (alpha0 * direction0 + alpha1 * direction1)[0:cases]
    res_ref[...] = (residual1 - alpha1 * along1)[0:cases]

    for copy in started:
        copy.wait_send()


def per_device(ny, nz, nx, nk, jump_data, lumped_scale, schur_inverse, coarse_coupling, corner_inverse, own_dof, nbr_dof, live_count, corner_index):
    cases, records = jump_data.shape[2:]
    corners, iface = coarse_coupling.shape[2:]
    total, block = corner_inverse.shape
    slabs = nx * nk
    wide = nx * LANES
    vmem = lambda *shape: pltpu.VMEM(shape, F32)
    half = lambda *shape: pltpu.VMEM(shape, BF16)
    whole = lambda *shape: pltpu.VMEM(shape, jnp.int32)
    sem = lambda *shape: pltpu.SemaphoreType.DMA(shape)
    in_vmem = pl.BlockSpec(memory_space=pltpu.VMEM)
    scratch = [
        vmem(iface, iface),
        vmem(total, block),
        half(iface, iface),
        half(iface, iface),
        half(iface, records),
        half(iface, records),
        half(block, wide),
        vmem(wide, block),
        half(wide, block),
        half(wide, block),
        vmem(LANES, iface),
        vmem(LANES, records),
        half(LANES, records),
        half(LANES, records),
        whole(ROWS, LANES),
        whole(ROWS, LANES),
        whole(ROWS, LANES),
        whole(slabs, ROWS, LANES),
        whole(nx, LANES),
        pltpu.SMEM((nx, LANES), jnp.int32),
        vmem(corners, iface),
        vmem(2, ROWS, iface),
        vmem(2, ROWS, iface),
        vmem(2, ROWS, iface),
        vmem(2, ROWS, iface),
        vmem(2, ROWS, LANES),
        vmem(2, slabs, ROWS, LANES),
        vmem(2, nx, ROWS, LANES),
        vmem(2, slabs, ROWS, LANES),
        vmem(ny, ROWS, block),
        vmem(nz, ROWS, block),
        vmem(ny, ROWS, 2 * block + LANES),
        vmem(nz, ROWS, 2 * block + LANES),
        sem(3),
        sem(6),
        sem(6),
        sem(slabs),
        sem(slabs),
        sem(2, slabs),
        sem(2, slabs),
        sem(2, slabs),
        sem(2, slabs),
        sem(2, ny),
        sem(2, ny),
        sem(2, nz),
        sem(2, nz),
    ]
    outs = pl.pallas_call(
        functools.partial(kernel, ny, nz, nx, nk),
        out_shape=(jax.ShapeDtypeStruct((cases, records), F32),) * 2,
        in_specs=[in_vmem] * 6
        + [pl.BlockSpec(memory_space=pltpu.SMEM), pl.BlockSpec(memory_space=pl.ANY), pl.BlockSpec(memory_space=pl.ANY)],
        out_specs=(in_vmem, in_vmem),
        scratch_shapes=scratch,
        compiler_params=pltpu.CompilerParams(collective_id=0, has_side_effects=True, vmem_limit_bytes=40 * 1024 * 1024),
        name="solve",
    )(
        jump_data[0, 0],
        lumped_scale[0],
        coarse_coupling[0, 0],
        own_dof[0],
        nbr_dof[0],
        corner_index[0],
        live_count,
        schur_inverse[0, 0],
        corner_inverse,
    )
    return outs[0][None, None], outs[1][None, None]


def solution(mesh):
    devices = mesh.devices
    sub, crs = devices.shape
    side = 8 if sub == 64 else 2
    ny, nz, nx, nk = side, sub // side, crs // 2, 2
    finer = Mesh(devices.reshape(ny, nz, nx, nk), ("y", "z", "x", "k"))
    SUB, CRS = ("y", "z"), ("x", "k")
    placed = (
        P(SUB, CRS, None, None),
        P(SUB, CRS, None),
        P(SUB, CRS, None, None),
        P(SUB, CRS, None, None),
        P(None, CRS),
        P(SUB, CRS, None),
        P(SUB, CRS, None),
        P(SUB, CRS),
        P(SUB, CRS, None),
    )
    return jax.shard_map(
        functools.partial(per_device, ny, nz, nx, nk),
        mesh=finer,
        in_specs=placed,
        out_specs=(P(SUB, CRS, None, None), P(SUB, CRS, None, None)),
        check_vma=False,
    )
```

time: 298 us -> 82.9 us (0.28)
  blocking collectives: 233 us -> 0 us
  Pallas kernels: 0 us -> 71.9 us
  waiting for transfers between devices: 22.9 us -> 0 us
  matrix products: 22 us -> 0 us
  starting transfers between devices: 13.8 us -> 0 us
  local copies, waits for them, and re-layouts: 1.38 us -> 9.35 us
    all_to_all x8 -> x0, blocking collectives: 129 us -> none  [the longest x6 97.4 us: copy_for_each(): return lax.all_to_all(copies, axis, split_axis=0, concat_axis=0, tiled=True)]
    psum x8 -> x0, blocking collectives: 103 us -> none  [over_axes(): value = lax.psum(value, axis)]
    pallas_call x0 -> x1, Pallas kernels: none -> 71.9 us  [per_device(): pl.pallas_call(functools.partial(kernel, ny, nz, nx, nk), out_shape=(jax....]
    ppermute x4 -> x0, waiting for transfers between devices: 22.9 us -> none  [passed_along(): return lax.ppermute(value, axis, pairs)]
    dot_general x20 -> x0, matrix products: 22 us -> none  [product(): jnp.dot(left, right, precision=lax.Precision.HIGHEST, preferred_element_t...]
    ppermute x4 -> x0, starting transfers between devices: 13.8 us -> none  [passed_along(): return lax.ppermute(value, axis, pairs)]
    unnamed x10 -> x17, local copies, waits for them, and re-layouts: 1.25 us -> 9.35 us
  transfers between devices with their start and end apart: 4 -> 0, of which waited for: 4 -> 0; matrix products, arithmetic and copies ran while one was open for 1% -> 0% of each run, Pallas kernels for 0% -> 0%
where the time goes in v1:
time: 82.9 us; the launch traced here: 82.5 us
  Pallas kernels  71.9 us (87%)
  local copies, waits for them, and re-layouts  9.35 us (11%)
  between operations  1.29 us (2%)
    pallas_call x1, Pallas kernels, per_device(): pl.pallas_call(functools.partial(kernel, ny, nz, nx, nk), out_shape=(jax....  71.9 us
    unnamed x17, local copies, waits for them, and re-layouts  9.35 us

profile of v1, /device:TPU:1, one launch (start us, length us, event | category | flops | bytes accessed | tf_op | source)
XLA Modules:
  0.0 82.5 jit_solution(1020472139298568091)
XLA Ops:
  1.3 0.7 copy.15
  2.0 0.0 copy-start
  2.0 2.2 %copy-done = f32[4096,256]{1,0:T(8,128)S(1)} copy-done((f32[4096,256]{1,0:T(8,128)S(1)}, f32[4096,256]{1,0:T(8,128)}, u32[]{:S(2)}) %copy-start) | copy-done | bytes 4194328
  4.2 0.0 copy-start.1
  4.2 1.7 %copy-done.1 = f32[1,1,768,768]{3,2,1,0:T(8,128)S(1)} copy-done((f32[1,1,768,768]{3,2,1,0:T(8,128)S(1)}, f32[1,1,768,768]{3,2,1,0:T(8,128)}, u32[]{:S(2)}) %copy-start.1) | copy-done | bytes 2359320
  5.8 0.0 copy-start.2
  5.8 0.9 %copy-done.2 = f32[1,1,24,768]{3,2,1,0:T(8,128)S(1)} copy-done((f32[1,1,24,768]{3,2,1,0:T(8,128)S(1)}, f32[1,1,24,768]{3,2,1,0:T(8,128)}, u32[]{:S(2)}) %copy-start.2) | copy-done | bytes 73752
  6.7 0.0 copy-start.3
  6.7 0.7 copy-done.3
  7.4 0.0 copy-start.4
  7.4 0.7 copy-done.4
  8.1 0.0 copy-start.5
  8.1 0.7 copy-done.5
  8.8 0.0 copy-start.6
  8.8 0.7 copy-done.6
  9.4 71.9 %solve.1 = (f32[6,384]{1,0:T(8,128)S(1)}, f32[6,384]{1,0:T(8,128)S(1)}) custom-call(f32[6,384]{1,0:T(8,128)S(1)} %bitcast.13, f32[1,384]{1,0:T(1,128)S(1)} %bitcast.16, f32[24,768]{1,0:T(8,128)S(1)} %bitcast.12, s32[1,384]{1,0:T(1,128)S(1)} %bitcast.17, s32[1,384]{1,0:T(1,128)S(1)} %bitcast.18, s32[1,24]{1,0:T(1,128)S(1)} %bitcast.19, ...), custom_call_target="tpu_custom_call" | custom-call | tf_op jit(solution)/shard_map/solve/pallas_call | solution.py:437
  81.3 0.6 copy.11
  81.9 0.6 copy.12
Async XLA Ops:
  2.0 2.2 %copy-start = (f32[4096,256]{1,0:T(8,128)S(1)}, f32[4096,256]{1,0:T(8,128)}, u32[]{:S(2)}) copy-start(f32[4096,256]{1,0:T(8,128)} %inverse_hbm.1) | copy-start | bytes 12582916
  4.2 1.7 %copy-start.1 = (f32[1,1,768,768]{3,2,1,0:T(8,128)S(1)}, f32[1,1,768,768]{3,2,1,0:T(8,128)}, u32[]{:S(2)}) copy-start(f32[1,1,768,768]{3,2,1,0:T(8,128)} %param.11) | copy-start | bytes 7077892
  5.8 0.9 %copy-start.2 = (f32[1,1,24,768]{3,2,1,0:T(8,128)S(1)}, f32[1,1,24,768]{3,2,1,0:T(8,128)}, u32[]{:S(2)}) copy-start(f32[1,1,24,768]{3,2,1,0:T(8,128)} %param.12) | copy-start | bytes 221188
  6.7 0.7 copy-start.3
  7.4 0.7 copy-start.4
  8.1 0.7 copy-start.5
  8.8 0.7 copy-start.6

commit v2 on v1

v2 whole, which is shorter than its diff:
```python
import functools

import jax
import jax.numpy as jnp
from jax import lax
from jax.experimental import pallas as pl
from jax.experimental.pallas import tpu as pltpu
from jax.sharding import Mesh
from jax.sharding import PartitionSpec as P

MESH = pl.DeviceIdType.MESH
LANES = 128
ROWS = 8
F32 = jnp.float32
BF16 = jnp.bfloat16
CONTRACT_LAST = (((1,), (1,)), ((), ()))
CONTRACT = (((1,), (0,)), ((), ()))


def parts(value):
    high = value.astype(BF16).astype(F32)
    rest = value - high
    middle = rest.astype(BF16).astype(F32)
    low = rest - middle
    return jnp.concatenate([high, middle, low], axis=0).astype(BF16)


def times(value, matrices, dims):
    rows = value.shape[0]
    stacked = parts(value)
    total = None
    for matrix in matrices:
        found = lax.dot_general(stacked, matrix, dims, preferred_element_type=F32)
        total = found if total is None else total + found
    return total[:rows] + total[rows : 2 * rows] + total[2 * rows :]


def store_split(value, high_ref, low_ref):
    high = value.astype(BF16)
    high_ref[...] = high
    low_ref[...] = (value - high.astype(F32)).astype(BF16)


def kernel(
    ny,
    nz,
    nx,
    nk,
    given_hbm,
    scale_hbm,
    coupling_hbm,
    own_hbm,
    nbr_hbm,
    index_hbm,
    live_ref,
    schur_hbm,
    inverse_hbm,
    mult_hbm,
    res_hbm,
    given_ref,
    scale_ref,
    coupling_ref,
    own_ref,
    nbr_ref,
    index_ref,
    mult_ref,
    res_ref,
    schur,
    inverse,
    schur_high,
    schur_low,
    own_map,
    next_map,
    corner_map,
    rows_of,
    rows_high,
    rows_low,
    own_wide,
    pair_wide,
    pair_high,
    pair_low,
    index_pad,
    index_right,
    index_mine,
    index_line,
    index_rows,
    index_smem,
    coupling_right,
    load_send,
    load_recv,
    disp_send,
    disp_recv,
    force_send,
    force_recv,
    pick_send,
    pick_recv,
    sum_y0,
    sum_z0,
    first_y,
    first_z,
    second_z,
    second_y,
    local_sem,
    near_send,
    near_recv,
    line_send,
    line_recv,
    axis_send,
    axis_recv,
    relay_sem,
):
    y, z, x, k = (lax.axis_index(a) for a in ("y", "z", "x", "k"))
    slab = x * nk + k
    slabs = nx * nk
    iface = coupling_ref.shape[1]
    corners = coupling_ref.shape[0]
    cases, _, records = given_ref.shape
    block = inverse.shape[1]
    half = LANES // nk

    def plus(value, step, count):
        return lax.rem(value + step + count, count)

    right_z = plus(z, 1, nz)
    right_y = plus(y, jnp.where(z == nz - 1, 1, 0), ny)
    left_z = plus(z, -1, nz)
    left_y = plus(y, jnp.where(z == 0, -1, 0), ny)
    right = {"y": right_y, "z": right_z}
    left = {"y": left_y, "z": left_z}

    def by_distance(count):
        return sorted(range(1, count), key=lambda d: -min(d, count - d))

    line = []
    for dx in sorted(range(nx), key=lambda d: -min(d, nx - d)):
        for dk in range(nk):
            if dx or dk:
                line.append((plus(x, dx, nx), plus(k, dk, nk)))
    ys = [plus(y, d, ny) for d in by_distance(ny)]
    zs = [plus(z, d, nz) for d in by_distance(nz)]

    aside = {
        "x": [{"x": plus(x, d, nx), "k": pk} for d in (-1, 1) for pk in range(nk)],
        "y": [{"y": plus(y, d, ny)} for d in (-1, 1)],
        "z": [{"z": plus(z, d, nz)} for d in (-1, 1)],
    }
    partners = [{"k": plus(k, d, nk)} for d in range(1, nk)]
    barrier = pltpu.get_barrier_semaphore()
    greeted = [left, right] + aside["x"] + aside["y"] + aside["z"] + partners
    for peer in greeted:
        pl.semaphore_signal(barrier, inc=1, device_id=peer, device_id_type=MESH)

    def relay_signal(axis, step):
        for peer in aside[axis]:
            pl.semaphore_signal(relay_sem.at["xyz".index(axis), step], inc=1, device_id=peer, device_id_type=MESH)

    def relay_wait(axis, step):
        pl.semaphore_wait(relay_sem.at["xyz".index(axis), step], len(aside[axis]))

    def relay(axis, count, first_step, last_step):
        for step in range(first_step, last_step):
            if step < count // 2 - 1:
                relay_wait(axis, step)
                if step + 1 < count // 2 - 1:
                    relay_signal(axis, step + 1)

    def fetch(source, target, slot):
        copy = pltpu.make_async_copy(source, target, local_sem.at[slot])
        copy.start()
        return copy

    get_nbr = fetch(nbr_hbm, nbr_ref, 3)
    get_given = fetch(given_hbm, given_ref, 4)
    get_scale = fetch(scale_hbm, scale_ref, 5)
    get_index = fetch(index_hbm, index_ref, 6)
    get_own = fetch(own_hbm, own_ref, 7)
    get_coupling = fetch(coupling_hbm, coupling_ref, 8)
    get_schur = fetch(schur_hbm, schur, 0)
    get_inverse = fetch(inverse_hbm, inverse, 1)

    unsent = []

    def send(source, target, send_sem, recv_sem, device):
        pltpu.make_async_remote_copy(
            src_ref=source,
            dst_ref=target,
            send_sem=send_sem,
            recv_sem=recv_sem,
            device_id=device,
            device_id_type=MESH,
        ).start()

    def bytes_of(view, send_sem, recv_sem):
        return pltpu.make_async_remote_copy(
            src_ref=view,
            dst_ref=view,
            send_sem=send_sem,
            recv_sem=recv_sem,
            device_id=right,
            device_id_type=MESH,
        )

    def send_near(source, target, slot, device):
        send(source, target, near_send.at[slot], near_recv.at[slot], device)
        unsent.append(bytes_of(source, near_send.at[slot], near_recv.at[slot]))

    def await_near(target, slot):
        bytes_of(target, near_send.at[slot], near_recv.at[slot]).wait_recv()

    def spread_line(source_of, target, rows, slot):
        for px, pk in line:
            send(
                source_of(px, pk),
                target.at[slab, 0:rows],
                line_send.at[slot],
                line_recv.at[slot],
                {"x": px, "k": pk},
            )
        unsent.append(bytes_of(target.at[0 : slabs - 1, 0:rows], line_send.at[slot], line_recv.at[slot]))

    def await_line(target, rows, slot):
        bytes_of(target.at[0 : slabs - 1, 0:rows], line_send.at[slot], line_recv.at[slot]).wait_recv()

    def spread_axis(buffer, axis, slot):
        me, peers = (y, ys) if axis == "y" else (z, zs)
        for peer in peers:
            send(buffer.at[me], buffer.at[me], axis_send.at[slot], axis_recv.at[slot], {axis: peer})
        unsent.append(bytes_of(buffer.at[0 : len(peers)], axis_send.at[slot], axis_recv.at[slot]))

    def await_axis(buffer, axis, slot):
        peers = ys if axis == "y" else zs
        bytes_of(buffer.at[0 : len(peers)], axis_send.at[slot], axis_recv.at[slot]).wait_recv()

    def added(buffer, count):
        total = buffer[0]
        for slot in range(1, count):
            total = total + buffer[slot]
        return total

    def padded(value):
        return jnp.concatenate([value, jnp.zeros((ROWS - value.shape[0], value.shape[1]), F32)], axis=0)

    live_row = lax.broadcasted_iota(jnp.int32, (1, records), 1) < live_ref[0, 0]
    rows_iface = lax.broadcasted_iota(jnp.int32, (iface, records), 0)
    get_nbr.wait()
    get_given.wait()
    get_scale.wait()
    given = jnp.concatenate([given_ref[i] for i in range(cases)], axis=0)
    residual0 = padded(given) * live_row.astype(F32)
    scale = scale_ref[...]
    direction0 = residual0 * scale
    next_map[...] = jnp.where((rows_iface == nbr_ref[...]) & live_row, 1.0, 0.0).astype(BF16)
    load_send[0] = times(direction0, (next_map[...],), CONTRACT_LAST)
    get_index.wait()
    index_pad[...] = jnp.full((ROWS, LANES), -1, jnp.int32)
    index_pad[0:1, 0:corners] = index_ref[...]

    get_own.wait()
    get_coupling.wait()
    pl.semaphore_wait(barrier, len(greeted))
    for axis, count in (("x", nx), ("y", ny), ("z", nz)):
        if count // 2 > 1:
            relay_signal(axis, 0)

    send_near(load_send.at[0], load_recv.at[0], 0, right)
    send_near(index_pad, index_right, 1, left)
    send_near(coupling_ref, coupling_right, 2, left)
    relay("x", nx, 0, 1)

    own_map[...] = jnp.where((rows_iface == own_ref[...]) & live_row, 1.0, 0.0).astype(BF16)
    own_load0 = times(direction0, (own_map[...],), CONTRACT_LAST)
    own_wide[...] = jnp.zeros_like(own_wide)
    pair_wide[...] = jnp.zeros_like(pair_wide)
    rows_of[...] = jnp.zeros_like(rows_of)
    coupling = coupling_ref[...]
    own_pair = times(coupling, (own_map[...],), CONTRACT)
    for at in range(0, LANES, half):
        own_wide[at : at + corners, :] = coupling
        pair_wide[at : at + corners, :] = own_pair
    wide_high = own_wide[...].astype(BF16)
    wide_low = (own_wide[...] - wide_high.astype(F32)).astype(BF16)
    relay("x", nx, 1, nx)

    await_near(index_right, 1)
    lane = lax.broadcasted_iota(jnp.int32, (ROWS, LANES), 1)
    row = lax.broadcasted_iota(jnp.int32, (ROWS, LANES), 0)
    low = lane < half
    both = jnp.where(lane < corners, index_pad[...], pltpu.roll(index_right[...], corners, 1))
    both = jnp.where(lane < 2 * corners, both, -1)
    index_mine[...] = jnp.where(low, both, pltpu.roll(both, half, 1))
    spread_line(lambda px, pk: index_mine.at[0:1], index_line, 1, 0)

    packed = cases // 2

    def up(tile):
        return pltpu.roll(tile, ROWS - packed, 0)

    def unpacked(tile):
        below = jnp.where((row < packed) & low, tile, 0.0)
        return jnp.where((row >= packed) & (row < cases) & ~low, pltpu.roll(tile, packed, 0), below)

    def send_force(step, force):
        force_send[step] = jnp.where(low, force, up(force))
        spread_line(lambda px, pk: force_send.at[step, 0:packed], force_recv.at[step], packed, 1 + 2 * step)

    await_near(load_recv.at[0], 0)
    load0 = own_load0 - load_recv[0]
    force = times(load0, (wide_high, wide_low), CONTRACT_LAST)
    send_force(0, force)
    relay("y", ny, 0, 1)
    relay("z", nz, 0, 1)

    get_schur.wait()
    store_split(schur[...], schur_high, schur_low)
    disp0 = times(load0, (schur_high[...], schur_low[...]), CONTRACT)
    disp_send[0] = disp0
    send_near(disp_send.at[0], disp_recv.at[0], 3, left)
    relay("y", ny, 1, ny)
    relay("z", nz, 1, 2)
    await_near(coupling_right, 2)
    next_pair = -times(coupling_right[...], (next_map[...],), CONTRACT)
    for at in range(corners, LANES, half):
        pair_wide[at : at + corners, :] = next_pair
    store_split(pair_wide[...], pair_high, pair_low)

    await_line(index_line, 1, 0)
    index_line[slab] = index_mine[...]
    block_rows = lax.broadcasted_iota(jnp.int32, (block, LANES), 0) + slab * block
    for px in range(nx):
        found = jnp.where(low, index_line[px * nk], index_line[px * nk + 1])[0:1]
        index_rows[px : px + 1, :] = found
        corner_map[:, px * LANES : (px + 1) * LANES] = jnp.where(block_rows == found, 1.0, 0.0).astype(BF16)
    to_smem = pltpu.make_async_copy(index_rows, index_smem, local_sem.at[2])
    to_smem.start()

    def line_force(step):
        await_line(force_recv.at[step], packed, 1 + 2 * step)
        force_recv[step, slab] = force_send[step]
        tiles = []
        for px in range(nx):
            even, odd = force_recv[step, px * nk], force_recv[step, px * nk + 1]
            upper = jnp.where(low, even, pltpu.roll(odd, half, 1))
            lower = pltpu.roll(jnp.where(low, pltpu.roll(even, half, 1), odd), packed, 0)
            tiles.append(jnp.where(row < packed, upper, jnp.where(row < cases, lower, 0.0)))
        return jnp.concatenate(tiles, axis=1)

    def send_picks(step, picks):
        for px in range(nx):
            tile = picks[:, px * LANES : (px + 1) * LANES]
            above = up(tile)
            pick_send[step, px, 0] = jnp.where(low, tile, pltpu.roll(above, half, 1))
            pick_send[step, px, 1] = jnp.where(low, pltpu.roll(tile, half, 1), above)
        spread_line(lambda px, pk: pick_send.at[step, px, pk, 0:packed], pick_recv.at[step], packed, 2 + 2 * step)
        pick_recv[step, slab] = pick_send[step, x, k]

    def get_picks(step):
        await_line(pick_recv.at[step], packed, 2 + 2 * step)
        return unpacked(added(pick_recv.at[step], slabs))

    sum_y0[y] = times(line_force(0), (corner_map[...],), CONTRACT_LAST)
    spread_axis(sum_y0, "y", 0)

    get_inverse.wait()
    to_smem.wait()

    def take(j, carry):
        for px in range(nx):
            for pk in range(nk):
                at = index_smem[px, pk * half + j]
                rows_of[pl.ds(px * LANES + pk * half + j, 1), :] = inverse[pl.ds(at, 1), :]
        return carry

    lax.fori_loop(0, 2 * corners, take, 0)
    store_split(rows_of[...], rows_high, rows_low)

    relay("z", nz, 2, nz)
    await_axis(sum_y0, "y", 0)
    sum_z0[z] = added(sum_y0, ny)
    spread_axis(sum_z0, "z", 1)
    await_near(disp_recv.at[0], 3)
    local0 = times(disp0, (own_map[...],), CONTRACT) - times(disp_recv[0], (next_map[...],), CONTRACT)
    await_axis(sum_z0, "z", 1)
    total0 = added(sum_z0, nz)
    send_picks(0, times(total0, (rows_high[...], rows_low[...]), CONTRACT_LAST))
    solved0 = get_picks(0)
    image0 = local0 + times(solved0, (pair_high[...], pair_low[...]), CONTRACT)

    scaled = image0 * scale
    load_send[1] = times(scaled, (next_map[...],), CONTRACT_LAST)
    send_near(load_send.at[1], load_recv.at[1], 4, right)
    send_force(1, times(scaled, (pair_high[...], pair_low[...]), CONTRACT_LAST))
    own_load1 = times(scaled, (own_map[...],), CONTRACT_LAST)

    def inner(first_value, second_value):
        return jnp.sum(first_value * second_value, axis=1, keepdims=True)

    start_norm = inner(residual0, direction0)
    curvature = inner(direction0, image0)
    scaled_norm = inner(image0, scaled)
    await_near(load_recv.at[1], 4)
    load1 = own_load1 - load_recv[1]
    disp1 = times(load1, (schur_high[...], schur_low[...]), CONTRACT)
    disp_send[1] = disp1
    send_near(disp_send.at[1], disp_recv.at[1], 5, left)
    energy = inner(load1, disp1)
    sums = jnp.where(
        lane == 0,
        start_norm,
        jnp.where(lane == 1, curvature, jnp.where(lane == 2, scaled_norm, jnp.where(lane == 3, energy, 0.0))),
    )
    forces = line_force(1)
    first_y[y, :, 0:block] = times(forces, (corner_map[...],), CONTRACT_LAST)
    first_y[y, :, block:] = sums
    spread_axis(first_y, "y", 2)
    first_z[z] = times(forces, (rows_high[...], rows_low[...]), CONTRACT)
    spread_axis(first_z, "z", 3)
    await_near(disp_recv.at[1], 5)
    local1 = times(disp1, (own_map[...],), CONTRACT) - times(disp_recv[1], (next_map[...],), CONTRACT)
    await_axis(first_y, "y", 2)
    second_z[z] = added(first_y, ny)
    spread_axis(second_z, "z", 4)
    await_axis(first_z, "z", 3)
    second_y[y] = added(first_z, nz)
    spread_axis(second_y, "y", 5)
    await_axis(second_y, "y", 5)
    solved_block = added(second_y, ny)
    picks = times(solved_block, (corner_map[...],), CONTRACT)
    await_axis(second_z, "z", 4)
    total1 = added(second_z, nz)
    sums = total1[:, block:]
    sums = sums + jnp.where(lane == 3, inner(total1[:, 0:block], solved_block), 0.0)
    spare = half - 16
    sums = pltpu.roll(sums, spare, 1) + pltpu.roll(sums, half + spare, 1)
    send_picks(1, picks + jnp.concatenate([sums] * nx, axis=1))
    solved1 = get_picks(1)
    image1 = local1 + times(solved1, (pair_high[...], pair_low[...]), CONTRACT)

    sums = solved1 + pltpu.roll(solved1, half, 1)
    norm0, curvature, scaled_norm, energy = (sums[:, spare + i : spare + i + 1] for i in range(4))
    alpha0 = norm0 / curvature
    norm1 = alpha0 * alpha0 * scaled_norm - norm0
    ratio = norm1 / norm0
    bent = alpha0 * alpha0 * energy - (norm0 + norm1) * (1.0 + ratio) / alpha0
    alpha1 = norm1 / bent
    residual1 = residual0 - alpha0 * image0
    direction1 = residual1 * scale + ratio * direction0
    along1 = image0 - alpha0 * image1 + ratio * image0
    mult = alpha0 * direction0 + alpha1 * direction1
    res = residual1 - alpha1 * along1
    for i in range(cases):
        mult_ref[i] = mult[i : i + 1]
        res_ref[i] = res[i : i + 1]
    puts = [fetch(mult_ref, mult_hbm, 9), fetch(res_ref, res_hbm, 10)]
    for put in puts:
        put.wait()

    for copy in unsent:
        copy.wait_send()


def per_device(ny, nz, nx, nk, jump_data, lumped_scale, schur_inverse, coarse_coupling, corner_inverse, own_dof, nbr_dof, live_count, corner_index):
    cases, records = jump_data.shape[2:]
    corners, iface = coarse_coupling.shape[2:]
    total, block = corner_inverse.shape
    slabs = nx * nk
    wide = nx * LANES
    vmem = lambda *shape: pltpu.VMEM(shape, F32)
    half = lambda *shape: pltpu.VMEM(shape, BF16)
    whole = lambda *shape: pltpu.VMEM(shape, jnp.int32)
    sem = lambda *shape: pltpu.SemaphoreType.DMA(shape)
    in_hbm = pl.BlockSpec(memory_space=pltpu.HBM)
    scratch = [
        vmem(cases, 1, records),
        vmem(1, records),
        vmem(corners, iface),
        whole(1, records),
        whole(1, records),
        whole(1, corners),
        vmem(cases, 1, records),
        vmem(cases, 1, records),
        vmem(iface, iface),
        vmem(total, block),
        half(iface, iface),
        half(iface, iface),
        half(iface, records),
        half(iface, records),
        half(block, wide),
        vmem(wide, block),
        half(wide, block),
        half(wide, block),
        vmem(LANES, iface),
        vmem(LANES, records),
        half(LANES, records),
        half(LANES, records),
        whole(ROWS, LANES),
        whole(ROWS, LANES),
        whole(ROWS, LANES),
        whole(slabs, ROWS, LANES),
        whole(nx, LANES),
        pltpu.SMEM((nx, LANES), jnp.int32),
        vmem(corners, iface),
        vmem(2, ROWS, iface),
        vmem(2, ROWS, iface),
        vmem(2, ROWS, iface),
        vmem(2, ROWS, iface),
        vmem(2, ROWS, LANES),
        vmem(2, slabs, ROWS, LANES),
        vmem(2, nx, nk, ROWS, LANES),
        vmem(2, slabs, ROWS, LANES),
        vmem(ny, ROWS, block),
        vmem(nz, ROWS, block),
        vmem(ny, ROWS, block + LANES),
        vmem(nz, ROWS, block),
        vmem(nz, ROWS, block + LANES),
        vmem(ny, ROWS, block),
        sem(11),
        sem(6),
        sem(6),
        sem(5),
        sem(5),
        sem(6),
        sem(6),
        pltpu.SemaphoreType.REGULAR((3, 4)),
    ]
    outs = pl.pallas_call(
        functools.partial(kernel, ny, nz, nx, nk),
        out_shape=(jax.ShapeDtypeStruct((cases, 1, records), F32),) * 2,
        in_specs=[in_hbm] * 6 + [pl.BlockSpec(memory_space=pltpu.SMEM)] + [in_hbm] * 2,
        out_specs=(in_hbm, in_hbm),
        scratch_shapes=scratch,
        compiler_params=pltpu.CompilerParams(collective_id=0, has_side_effects=True, vmem_limit_bytes=67043328),
        name="solve",
    )(
        jnp.transpose(jump_data[0], (1, 0, 2)),
        lumped_scale[0],
        coarse_coupling[0, 0],
        own_dof[0],
        nbr_dof[0],
        corner_index[0],
        live_count,
        schur_inverse[0, 0],
        corner_inverse,
    )
    return tuple(jnp.transpose(out, (1, 0, 2))[None] for out in outs)


def solution(mesh):
    devices = mesh.devices
    sub, crs = devices.shape
    side = 8 if sub == 64 else 2
    ny, nz, nx, nk = side, sub // side, crs // 2, 2
    finer = Mesh(devices.reshape(ny, nz, nx, nk), ("y", "z", "x", "k"))
    SUB, CRS = ("y", "z"), ("x", "k")
    placed = (
        P(SUB, CRS, None, None),
        P(SUB, CRS, None),
        P(SUB, CRS, None, None),
        P(SUB, CRS, None, None),
        P(None, CRS),
        P(SUB, CRS, None),
        P(SUB, CRS, None),
        P(SUB, CRS),
        P(SUB, CRS, None),
    )
    return jax.shard_map(
        functools.partial(per_device, ny, nz, nx, nk),
        mesh=finer,
        in_specs=placed,
        out_specs=(P(SUB, CRS, None, None), P(SUB, CRS, None, None)),
        check_vma=False,
    )
```

time: 82.9 us -> 72.5 us (0.87)
  local copies, waits for them, and re-layouts: 9.35 us -> 2.6 us
  Pallas kernels: 71.9 us -> 68.3 us
    unnamed x17 -> x2, local copies, waits for them, and re-layouts: 9.35 us -> 2.6 us
    pallas_call x1, Pallas kernels: 71.9 us -> 68.3 us  [per_device(): pl.pallas_call(functools.partial(kernel, ny, nz, nx, nk), out_shape=(jax....]
where the time goes in v2:
time: 72.5 us; the launch traced here: 72.2 us
  Pallas kernels  68.3 us (94%)
  local copies, waits for them, and re-layouts  2.6 us (4%)
  between operations  1.29 us (2%)
    pallas_call x1, Pallas kernels, per_device(): pl.pallas_call(functools.partial(kernel, ny, nz, nx, nk), out_shape=(jax....  68.3 us
    unnamed x2, local copies, waits for them, and re-layouts  2.6 us

profile of v2, /device:TPU:1, one launch (start us, length us, event | category | flops | bytes accessed | tf_op | source)
XLA Modules:
  0.0 72.2 jit_solution(3482322079106317286)
XLA Ops:
  1.3 68.3 %solve.1 = (f32[6,1,384]{2,1,0:T(1,128)}, f32[6,1,384]{2,1,0:T(1,128)}) custom-call(f32[6,1,384]{2,1,0:T(1,128)} %bitcast.17, f32[1,384]{1,0:T(1,128)} %bitcast.18, f32[24,768]{1,0:T(8,128)} %bitcast.14, s32[1,384]{1,0:T(1,128)} %bitcast.19, s32[1,384]{1,0:T(1,128)} %bitcast.20, s32[1,24]{1,0:T(1,128)} %bitcast.21, s32[1,1]{1,0:T(1,128)S(6)} %copy.15.live_ref, ...), custom_call_target="tpu_custom_call" | custom-call | tf_op jit(solution)/shard_map/solve/pallas_call | solution.py:525
  69.6 1.3 %copy.16 = f32[1,1,6,384]{3,1,2,0:T(1,128)} copy(f32[1,1,6,384]{3,1,2,0:T(1,128)} %bitcast.16) | data formatting | bytes 18432
  70.9 1.3 %copy.17 = f32[1,1,6,384]{3,1,2,0:T(1,128)} copy(f32[1,1,6,384]{3,1,2,0:T(1,128)} %bitcast.15) | data formatting | bytes 18432

commit v3 on v2

--- a/solution.py
+++ b/solution.py
@@ -55,16 +55,14 @@
     live_ref,
     schur_hbm,
     inverse_hbm,
-    mult_hbm,
-    res_hbm,
+    out_hbm,
     given_ref,
     scale_ref,
     coupling_ref,
     own_ref,
     nbr_ref,
     index_ref,
-    mult_ref,
-    res_ref,
+    out_ref,
     schur,
     inverse,
     schur_high,
@@ -224,12 +222,12 @@
     def spread_axis(buffer, axis, slot):
         me, peers = (y, ys) if axis == "y" else (z, zs)
         for peer in peers:
-            send(buffer.at[me], buffer.at[me], axis_send.at[slot], axis_recv.at[slot], {axis: peer})
-        unsent.append(bytes_of(buffer.at[0 : len(peers)], axis_send.at[slot], axis_recv.at[slot]))
+            send(buffer.at[me, 0:cases], buffer.at[me, 0:cases], axis_send.at[slot], axis_recv.at[slot], {axis: peer})
+        unsent.append(bytes_of(buffer.at[0 : len(peers), 0:cases], axis_send.at[slot], axis_recv.at[slot]))
 
     def await_axis(buffer, axis, slot):
         peers = ys if axis == "y" else zs
-        bytes_of(buffer.at[0 : len(peers)], axis_send.at[slot], axis_recv.at[slot]).wait_recv()
+        bytes_of(buffer.at[0 : len(peers), 0:cases], axis_send.at[slot], axis_recv.at[slot]).wait_recv()
 
     def added(buffer, count):
         total = buffer[0]
@@ -240,8 +238,8 @@
     def padded(value):
         return jnp.concatenate([value, jnp.zeros((ROWS - value.shape[0], value.shape[1]), F32)], axis=0)
 
+    rows_iface = lax.broadcasted_iota(jnp.int32, (iface, records), 0)
     live_row = lax.broadcasted_iota(jnp.int32, (1, records), 1) < live_ref[0, 0]
-    rows_iface = lax.broadcasted_iota(jnp.int32, (iface, records), 0)
     get_nbr.wait()
     get_given.wait()
     get_scale.wait()
@@ -262,8 +260,8 @@
         if count // 2 > 1:
             relay_signal(axis, 0)
 
-    send_near(load_send.at[0], load_recv.at[0], 0, right)
-    send_near(index_pad, index_right, 1, left)
+    send_near(load_send.at[0, 0:cases], load_recv.at[0, 0:cases], 0, right)
+    send_near(index_pad.at[0:1], index_right.at[0:1], 1, left)
     send_near(coupling_ref, coupling_right, 2, left)
     relay("x", nx, 0, 1)
 
@@ -281,7 +279,7 @@
     wide_low = (own_wide[...] - wide_high.astype(F32)).astype(BF16)
     relay("x", nx, 1, nx)
 
-    await_near(index_right, 1)
+    await_near(index_right.at[0:1], 1)
     lane = lax.broadcasted_iota(jnp.int32, (ROWS, LANES), 1)
     row = lax.broadcasted_iota(jnp.int32, (ROWS, LANES), 0)
     low = lane < half
@@ -303,7 +301,7 @@
         force_send[step] = jnp.where(low, force, up(force))
         spread_line(lambda px, pk: force_send.at[step, 0:packed], force_recv.at[step], packed, 1 + 2 * step)
 
-    await_near(load_recv.at[0], 0)
+    await_near(load_recv.at[0, 0:cases], 0)
     load0 = own_load0 - load_recv[0]
     force = times(load0, (wide_high, wide_low), CONTRACT_LAST)
     send_force(0, force)
@@ -314,7 +312,7 @@
     store_split(schur[...], schur_high, schur_low)
     disp0 = times(load0, (schur_high[...], schur_low[...]), CONTRACT)
     disp_send[0] = disp0
-    send_near(disp_send.at[0], disp_recv.at[0], 3, left)
+    send_near(disp_send.at[0, 0:cases], disp_recv.at[0, 0:cases], 3, left)
     relay("y", ny, 1, ny)
     relay("z", nz, 1, 2)
     await_near(coupling_right, 2)
@@ -370,14 +368,14 @@
                 rows_of[pl.ds(px * LANES + pk * half + j, 1), :] = inverse[pl.ds(at, 1), :]
         return carry
 
-    lax.fori_loop(0, 2 * corners, take, 0)
-    store_split(rows_of[...], rows_high, rows_low)
-
+    lax.fori_loop(0, corners, take, 0)
     relay("z", nz, 2, nz)
     await_axis(sum_y0, "y", 0)
     sum_z0[z] = added(sum_y0, ny)
     spread_axis(sum_z0, "z", 1)
-    await_near(disp_recv.at[0], 3)
+    await_near(disp_recv.at[0, 0:cases], 3)
+    lax.fori_loop(corners, 2 * corners, take, 0)
+    store_split(rows_of[...], rows_high, rows_low)
     local0 = times(disp0, (own_map[...],), CONTRACT) - times(disp_recv[0], (next_map[...],), CONTRACT)
     await_axis(sum_z0, "z", 1)
     total0 = added(sum_z0, nz)
@@ -386,9 +384,9 @@
     image0 = local0 + times(solved0, (pair_high[...], pair_low[...]), CONTRACT)
 
     scaled = image0 * scale
+    send_force(1, times(scaled, (pair_high[...], pair_low[...]), CONTRACT_LAST))
     load_send[1] = times(scaled, (next_map[...],), CONTRACT_LAST)
-    send_near(load_send.at[1], load_recv.at[1], 4, right)
-    send_force(1, times(scaled, (pair_high[...], pair_low[...]), CONTRACT_LAST))
+    send_near(load_send.at[1, 0:cases], load_recv.at[1, 0:cases], 4, right)
     own_load1 = times(scaled, (own_map[...],), CONTRACT_LAST)
 
     def inner(first_value, second_value):
@@ -397,11 +395,11 @@
     start_norm = inner(residual0, direction0)
     curvature = inner(direction0, image0)
     scaled_norm = inner(image0, scaled)
-    await_near(load_recv.at[1], 4)
+    await_near(load_recv.at[1, 0:cases], 4)
     load1 = own_load1 - load_recv[1]
     disp1 = times(load1, (schur_high[...], schur_low[...]), CONTRACT)
     disp_send[1] = disp1
-    send_near(disp_send.at[1], disp_recv.at[1], 5, left)
+    send_near(disp_send.at[1, 0:cases], disp_recv.at[1, 0:cases], 5, left)
     energy = inner(load1, disp1)
     sums = jnp.where(
         lane == 0,
@@ -414,7 +412,7 @@
     spread_axis(first_y, "y", 2)
     first_z[z] = times(forces, (rows_high[...], rows_low[...]), CONTRACT)
     spread_axis(first_z, "z", 3)
-    await_near(disp_recv.at[1], 5)
+    await_near(disp_recv.at[1, 0:cases], 5)
     local1 = times(disp1, (own_map[...],), CONTRACT) - times(disp_recv[1], (next_map[...],), CONTRACT)
     await_axis(first_y, "y", 2)
     second_z[z] = added(first_y, ny)
@@ -448,11 +446,10 @@
     mult = alpha0 * direction0 + alpha1 * direction1
     res = residual1 - alpha1 * along1
     for i in range(cases):
-        mult_ref[i] = mult[i : i + 1]
-        res_ref[i] = res[i : i + 1]
-    puts = [fetch(mult_ref, mult_hbm, 9), fetch(res_ref, res_hbm, 10)]
-    for put in puts:
-        put.wait()
+        out_ref[0, i] = mult[i : i + 1]
+        out_ref[1, i] = res[i : i + 1]
+    put = fetch(out_ref, out_hbm, 9)
+    put.wait()
 
     for copy in unsent:
         copy.wait_send()
@@ -476,8 +473,7 @@
         whole(1, records),
         whole(1, records),
         whole(1, corners),
-        vmem(cases, 1, records),
-        vmem(cases, 1, records),
+        vmem(2, cases, 1, records),
         vmem(iface, iface),
         vmem(total, block),
         half(iface, iface),
@@ -524,9 +520,9 @@
     ]
     outs = pl.pallas_call(
         functools.partial(kernel, ny, nz, nx, nk),
-        out_shape=(jax.ShapeDtypeStruct((cases, 1, records), F32),) * 2,
+        out_shape=jax.ShapeDtypeStruct((2, cases, 1, records), F32),
         in_specs=[in_hbm] * 6 + [pl.BlockSpec(memory_space=pltpu.SMEM)] + [in_hbm] * 2,
-        out_specs=(in_hbm, in_hbm),
+        out_specs=in_hbm,
         scratch_shapes=scratch,
         compiler_params=pltpu.CompilerParams(collective_id=0, has_side_effects=True, vmem_limit_bytes=67043328),
         name="solve",
@@ -541,7 +537,7 @@
         schur_inverse[0, 0],
         corner_inverse,
     )
-    return tuple(jnp.transpose(out, (1, 0, 2))[None] for out in outs)
+    return tuple(jnp.transpose(outs[i], (1, 0, 2))[None] for i in range(2))
 
 
 def solution(mesh):

time: 72.5 us -> 70.5 us (0.972)
  local copies, waits for them, and re-layouts: 2.6 us -> 1.33 us
    unnamed x2 -> x1, local copies, waits for them, and re-layouts: 2.6 us -> 1.33 us
where the time goes in v3:
time: 70.5 us; the launch traced here: 70.3 us
  Pallas kernels  67.7 us (96%)
  local copies, waits for them, and re-layouts  1.33 us (2%)
  between operations  1.29 us (2%)
    pallas_call x1, Pallas kernels, per_device(): pl.pallas_call(functools.partial(kernel, ny, nz, nx, nk), out_shape=jax.S...  67.7 us

profile of v3, /device:TPU:1, one launch (start us, length us, event | category | flops | bytes accessed | tf_op | source)
XLA Modules:
  0.0 70.3 jit_solution(18016685317902951233)
XLA Ops:
  1.3 67.7 %solve.1 = f32[2,6,1,384]{3,2,1,0:T(1,128)} custom-call(f32[6,1,384]{2,1,0:T(1,128)} %bitcast.17, f32[1,384]{1,0:T(1,128)} %bitcast.18, f32[24,768]{1,0:T(8,128)} %bitcast.16, s32[1,384]{1,0:T(1,128)} %bitcast.19, s32[1,384]{1,0:T(1,128)} %bitcast.20, s32[1,24]{1,0:T(1,128)} %bitcast.21, s32[1,1]{1,0:T(1,128)S(6)} %copy.13.live_ref, f32[768,768]{1,0:T(8,128)} %bitcast.15, ...), custom_call_target="tpu_custom_call" | custom-call | tf_op jit(solution)/shard_map/solve/pallas_call | solution.py:521
  69.0 1.3 %slice_bitcast_fusion = (f32[1,1,6,384]{3,1,2,0:T(1,128)}, f32[1,1,6,384]{3,1,2,0:T(1,128)}) fusion(f32[2,6,1,384]{3,2,1,0:T(1,128)} %solve.1), kind=kLoop, calls=%fused_computation | loop fusion | bytes 36864

commit v4 on v3

--- a/solution.py
+++ b/solution.py
@@ -173,8 +173,6 @@
     get_index = fetch(index_hbm, index_ref, 6)
     get_own = fetch(own_hbm, own_ref, 7)
     get_coupling = fetch(coupling_hbm, coupling_ref, 8)
-    get_schur = fetch(schur_hbm, schur, 0)
-    get_inverse = fetch(inverse_hbm, inverse, 1)
 
     unsent = []
 
@@ -305,6 +303,8 @@
     load0 = own_load0 - load_recv[0]
     force = times(load0, (wide_high, wide_low), CONTRACT_LAST)
     send_force(0, force)
+    get_schur = fetch(schur_hbm, schur, 0)
+    get_inverse = fetch(inverse_hbm, inverse, 1)
     relay("y", ny, 0, 1)
     relay("z", nz, 0, 1)
 

time: 70.5 us -> 70.7 us (level)
  no operation moved by 1% of the time
where the time goes in v4:
time: 70.7 us; the launch traced here: 70.4 us
  Pallas kernels  67.8 us (96%)
  local copies, waits for them, and re-layouts  1.33 us (2%)
  between operations  1.29 us (2%)
    pallas_call x1, Pallas kernels, per_device(): pl.pallas_call(functools.partial(kernel, ny, nz, nx, nk), out_shape=jax.S...  67.8 us

profile of v4, /device:TPU:1, one launch (start us, length us, event | category | flops | bytes accessed | tf_op | source)
XLA Modules:
  0.0 70.4 jit_solution(10321847733841453114)
XLA Ops:
  1.3 67.8 %solve.1 = f32[2,6,1,384]{3,2,1,0:T(1,128)} custom-call(f32[6,1,384]{2,1,0:T(1,128)} %bitcast.17, f32[1,384]{1,0:T(1,128)} %bitcast.18, f32[24,768]{1,0:T(8,128)} %bitcast.16, s32[1,384]{1,0:T(1,128)} %bitcast.19, s32[1,384]{1,0:T(1,128)} %bitcast.20, s32[1,24]{1,0:T(1,128)} %bitcast.21, s32[1,1]{1,0:T(1,128)S(6)} %copy.13.live_ref, f32[768,768]{1,0:T(8,128)} %bitcast.15, ...), custom_call_target="tpu_custom_call" | custom-call | tf_op jit(solution)/shard_map/solve/pallas_call | solution.py:521
  69.1 1.3 %slice_bitcast_fusion = (f32[1,1,6,384]{3,1,2,0:T(1,128)}, f32[1,1,6,384]{3,1,2,0:T(1,128)}) fusion(f32[2,6,1,384]{3,2,1,0:T(1,128)} %solve.1), kind=kLoop, calls=%fused_computation | loop fusion | bytes 36864
